TPU v7x, 32 devices: a whole 2x2x4 slice. The times are simulated.
32 devices in a mesh: shard: 8 (over z, x), rep: 4 (over y, core).
Axes of the slice: x: 2, y: 2, z: 4, core: 2. Of those that a mesh axis runs over, the one named last changes fastest.
Arguments:
- images: bfloat16 [32, 197, 768], P(('shard', 'rep')), may hold values from -6 to 6
- cotangent: bfloat16 [32, 197, 768], P(('shard', 'rep')), may hold values from -6 to 6
- weights_in: float32 [768, 6144], P('shard'), may hold values from -13 to 13
- weights_down: float32 [3072, 768], P('shard'), may hold values from -0.109375 to 0.109375
- vectors: float32 [12, 768], P(None, 'shard'), may hold values from -1.5 to 1.5, as said below
- mean_in: float32 [768, 6144], P('shard'), may hold values from -256 to 256
- mean_down: float32 [3072, 768], P('shard'), may hold values from -256 to 256
- mean_vectors: float32 [12, 768], P(None, 'shard'), may hold values from -256 to 256
- square_in: float32 [768, 6144], P('shard'), may hold values from 63.04 to 6304
- square_down: float32 [3072, 768], P('shard'), may hold values from 63.04 to 6304
- square_vectors: float32 [12, 768], P(None, 'shard'), may hold values from 63.04 to 6304
Outputs:
- block_out: bfloat16 [32, 197, 768], P(('shard', 'rep'))
- input_grad: float32 [32, 197, 768], P(('shard', 'rep'))
- grad_in: float32 [768, 6144], P('shard')
- grad_down: float32 [3072, 768], P('shard')
- grad_vectors: float32 [12, 768], P(None, 'shard')
- updated_in: float32 [768, 6144], P('shard')
- updated_down: float32 [3072, 768], P('shard')
- updated_vectors: float32 [12, 768], P(None, 'shard')
- next_mean_in: float32 [768, 6144], P('shard')
- next_mean_down: float32 [3072, 768], P('shard')
- next_mean_vectors: float32 [12, 768], P(None, 'shard')
- next_square_in: float32 [768, 6144], P('shard')
- next_square_down: float32 [3072, 768], P('shard')
- next_square_vectors: float32 [12, 768], P(None, 'shard')
Inputs may be any that keep to these rules, and one draw needn't show every extreme that they name: `vectors`: rows 0 and 5 are the norms' gains.
All inputs are finite; a program needn't handle non-finite values.
Results may differ from a plain program's by a relative error of at most 0.023.
Values may be sent and summed in bfloat16 or wider, within the bound.
A program may use at most 128 MiB of HBM per device.

v0:
```python
import math
import jax
import jax.numpy as jnp
from jax import lax
from jax.sharding import PartitionSpec as P

HEADS = 12
NORM_EPS = 1e-06
BETA_ONE = 0.9
BETA_TWO = 0.95
ADAM_EPS = 1e-08
RATE_MATRIX = 0.008
RATE_VECTOR = 0.15
DECAY_MATRIX = 0.05
STEP_COUNT = 2.0


def to_half(array_in):
    return array_in.astype(jnp.bfloat16)


def matmul(left, right):
    return jnp.dot(left, right, preferred_element_type=jnp.float32)


def times_transposed(left, right):
    return lax.dot_general(
        left, right, (((1,), (1,)), ((), ())), preferred_element_type=jnp.float32
    )


def transposed_times(left, right):
    return lax.dot_general(
        left, right, (((0,), (0,)), ((), ())), preferred_element_type=jnp.float32
    )


def layer_norm(inputs, gain, shift):
    centred = inputs - jnp.mean(inputs, axis=-1, keepdims=True)
    inv_std = lax.rsqrt(jnp.mean(centred * centred, axis=-1, keepdims=True) + NORM_EPS)
    normed = centred * inv_std
    return (normed, inv_std, normed * gain + shift)


def norm_back(grad_after, normed, inv_std, gain):
    grad_normed = grad_after * gain
    grad_inputs = inv_std * (
        grad_normed
        - jnp.mean(grad_normed, axis=-1, keepdims=True)
        - normed * jnp.mean(grad_normed * normed, axis=-1, keepdims=True)
    )
    return (grad_inputs, jnp.sum(grad_after * normed, axis=0), jnp.sum(grad_after, axis=0))


def gaussian_unit(hidden):
    cdf_part = 0.5 * (1.0 + jax.scipy.special.erf(hidden * 0.7071067811865476))
    slope = cdf_part + hidden * jnp.exp(-0.5 * hidden * hidden) * 0.3989422804014327
    return (hidden * cdf_part, slope)


def head_scores(query_heads, key_heads, score_scale):
    return (
        jnp.einsum("bqhe,bkhe->bhqk", query_heads, key_heads, preferred_element_type=jnp.float32)
        * score_scale
    )


def forward_pass(images, matrix_half, down_half, vector_half):
    img_count, seq_len, model_width = images.shape
    head_dim = model_width // HEADS
    score_scale = 1.0 / math.sqrt(head_dim)
    row_count = img_count * seq_len
    head_shape = (img_count, seq_len, HEADS, head_dim)
    vector_float = vector_half.astype(jnp.float32)
    flat_in = images.reshape(row_count, model_width).astype(jnp.float32)
    normed_one, inv_one, pre_one = layer_norm(flat_in, vector_float[0], vector_float[1])
    act_one = to_half(pre_one)
    projected = matmul(act_one, matrix_half[:, : 3 * model_width])
    query_heads = to_half(projected[:, :model_width] + vector_float[2]).reshape(head_shape)
    key_heads = to_half(projected[:, model_width : 2 * model_width]).reshape(head_shape)
    value_heads = to_half(projected[:, 2 * model_width :] + vector_float[3]).reshape(head_shape)
    scores = head_scores(query_heads, key_heads, score_scale)
    log_total = jax.nn.logsumexp(scores, axis=-1, keepdims=True)
    probs_half = to_half(jnp.exp(scores - log_total))
    attended = to_half(
        jnp.einsum(
            "bhqk,bkhe->bqhe", probs_half, value_heads, preferred_element_type=jnp.float32
        ).reshape(row_count, model_width)
    )
    hidden_one = (
        flat_in
        + matmul(attended, matrix_half[:, 3 * model_width : 4 * model_width])
        + vector_float[4]
    )
    normed_two, inv_two, pre_two = layer_norm(hidden_one, vector_float[5], vector_float[6])
    act_two = to_half(pre_two)
    up_input = matmul(act_two, matrix_half[:, 4 * model_width :]) + vector_float[8:].reshape(-1)
    gelu_out, gelu_slope = gaussian_unit(up_input)
    gelu_half = to_half(gelu_out)
    block_out = to_half(hidden_one + matmul(gelu_half, down_half) + vector_float[7])
    saved = (
        normed_one,
        inv_one,
        act_one,
        query_heads,
        key_heads,
        value_heads,
        log_total,
        attended,
        normed_two,
        inv_two,
        act_two,
        gelu_slope,
        gelu_half,
    )
    return (block_out.reshape(images.shape), saved)


def backward_pass(cotangent, saved, matrix_half, down_half, vector_half):
    (
        normed_one,
        inv_one,
        act_one,
        query_heads,
        key_heads,
        value_heads,
        log_total,
        attended,
        normed_two,
        inv_two,
        act_two,
        gelu_slope,
        gelu_half,
    ) = saved
    img_count, seq_len, model_width = cotangent.shape
    head_dim = model_width // HEADS
    score_scale = 1.0 / math.sqrt(head_dim)
    row_count = img_count * seq_len
    head_shape = (img_count, seq_len, HEADS, head_dim)
    vector_float = vector_half.astype(jnp.float32)
    joint_weights = matrix_half[:, : 3 * model_width]
    output_weights = matrix_half[:, 3 * model_width : 4 * model_width]
    upward_weights = matrix_half[:, 4 * model_width :]
    grad_half = cotangent.reshape(row_count, model_width)
    grad_out = grad_half.astype(jnp.float32)
    grad_up = times_transposed(grad_half, down_half) * gelu_slope
    up_half = to_half(grad_up)
    grad_act_two = times_transposed(up_half, upward_weights)
    grad_norm_two, grad_gain_two, grad_shift_two = norm_back(
        grad_act_two, normed_two, inv_two, vector_float[5]
    )
    grad_hidden = grad_out + grad_norm_two
    hidden_half = to_half(grad_hidden)
    grad_att = to_half(times_transposed(hidden_half, output_weights)).reshape(head_shape)
    prob_float = jnp.exp(head_scores(query_heads, key_heads, score_scale) - log_total)
    probs_half = to_half(prob_float)
    grad_probs = jnp.einsum(
        "bqhe,bkhe->bhqk", grad_att, value_heads, preferred_element_type=jnp.float32
    )
    row_inner = jnp.sum(prob_float * grad_probs, axis=-1, keepdims=True)
    grad_scores = to_half(prob_float * (grad_probs - row_inner) * score_scale)
    grad_query = jnp.einsum(
        "bhqk,bkhe->bqhe", grad_scores, key_heads, preferred_element_type=jnp.float32
    ).reshape(row_count, model_width)
    grad_key = jnp.einsum(
        "bhqk,bqhe->bkhe", grad_scores, query_heads, preferred_element_type=jnp.float32
    ).reshape(row_count, model_width)
    grad_value = jnp.einsum(
        "bhqk,bqhe->bkhe", probs_half, grad_att, preferred_element_type=jnp.float32
    ).reshape(row_count, model_width)
    grad_proj = to_half(jnp.concatenate([grad_query, grad_key, grad_value], axis=1))
    grad_act_one = times_transposed(grad_proj, joint_weights)
    grad_norm_one, grad_gain_one, grad_shift_one = norm_back(
        grad_act_one, normed_one, inv_one, vector_float[0]
    )
    input_grad = (grad_hidden + grad_norm_one).reshape(cotangent.shape)
    grad_down = transposed_times(gelu_half, grad_half)
    small_rows = jnp.stack(
        [
            grad_gain_one,
            grad_shift_one,
            jnp.sum(grad_query, axis=0),
            jnp.sum(grad_value, axis=0),
            jnp.sum(grad_hidden, axis=0),
            grad_gain_two,
            grad_shift_two,
            jnp.sum(grad_out, axis=0),
        ]
    )
    grad_vectors = jnp.concatenate(
        [small_rows, jnp.sum(grad_up, axis=0).reshape(4, model_width)], axis=0
    )
    factors = (act_one, grad_proj, attended, hidden_half, act_two, up_half)
    return (input_grad, grad_down, grad_vectors, factors)


def adam_update(weights, first, second, gradient, rate, decay):
    next_first = BETA_ONE * first + (1.0 - BETA_ONE) * gradient
    next_second = BETA_TWO * second + (1.0 - BETA_TWO) * gradient * gradient
    corr_first = next_first / (1.0 - BETA_ONE**STEP_COUNT)
    corr_second = next_second / (1.0 - BETA_TWO**STEP_COUNT)
    updated = weights - rate * (corr_first / (jnp.sqrt(corr_second) + ADAM_EPS) + decay * weights)
    return (updated, next_first, next_second)


def local(
    images,
    cotangent,
    weights_in,
    weights_down,
    vectors,
    mean_in,
    mean_down,
    mean_vectors,
    square_in,
    square_down,
    square_vectors,
):
    halves = (to_half(weights_in), to_half(weights_down), to_half(vectors))
    forward_set = (
        lax.all_gather(halves[0], "shard", axis=0, tiled=True),
        lax.all_gather(halves[1], "shard", axis=0, tiled=True),
        lax.all_gather(halves[2], "shard", axis=1, tiled=True),
    )
    block_out, saved = forward_pass(images, forward_set[0], forward_set[1], forward_set[2])
    backward_set = (
        lax.all_gather(halves[0], "shard", axis=0, tiled=True),
        lax.all_gather(halves[1], "shard", axis=0, tiled=True),
        lax.all_gather(halves[2], "shard", axis=1, tiled=True),
    )
    input_grad, grad_down_local, grad_vectors_local, factors = backward_pass(
        cotangent, saved, backward_set[0], backward_set[1], backward_set[2]
    )
    act_one, grad_proj, attended, hidden_half, act_two, up_half = factors

    def column_part(activation, gradient):
        return transposed_times(activation, gradient)

    owned_in = lax.psum_scatter(
        jnp.concatenate(
            [
                column_part(act_one, grad_proj),
                column_part(attended, hidden_half),
                column_part(act_two, up_half),
            ],
            axis=1,
        ).astype(jnp.bfloat16),
        "shard",
        scatter_dimension=0,
        tiled=True,
    )
    owned_down, owned_vectors = (
        lax.psum_scatter(
            grad_down_local.astype(jnp.bfloat16), "shard", scatter_dimension=0, tiled=True
        ).astype(jnp.float32),
        lax.psum_scatter(
            grad_vectors_local.astype(jnp.bfloat16), "shard", scatter_dimension=1, tiled=True
        ).astype(jnp.float32),
    )
    grad_in, grad_down, grad_vectors = (
        lax.psum(owned_in, "rep").astype(jnp.float32),
        lax.psum(owned_down.astype(jnp.bfloat16), "rep").astype(jnp.float32),
        lax.psum(owned_vectors.astype(jnp.bfloat16), "rep").astype(jnp.float32),
    )
    new_in = adam_update(weights_in, mean_in, square_in, grad_in, RATE_MATRIX, DECAY_MATRIX)
    new_down = adam_update(
        weights_down, mean_down, square_down, grad_down, RATE_MATRIX, DECAY_MATRIX
    )
    new_vectors = adam_update(vectors, mean_vectors, square_vectors, grad_vectors, RATE_VECTOR, 0.0)
    return (
        block_out,
        input_grad,
        grad_in,
        grad_down,
        grad_vectors,
        new_in[0],
        new_down[0],
        new_vectors[0],
        new_in[1],
        new_down[1],
        new_vectors[1],
        new_in[2],
        new_down[2],
        new_vectors[2],
    )


def solution(mesh):
    placed = (
        P(("shard", "rep"), None, None),
        P(("shard", "rep"), None, None),
        P("shard", None),
        P("shard", None),
        P(None, "shard"),
        P("shard", None),
        P("shard", None),
        P(None, "shard"),
        P("shard", None),
        P("shard", None),
        P(None, "shard"),
    )
    return jax.shard_map(
        local,
        mesh=mesh,
        in_specs=placed,
        out_specs=(
            P(("shard", "rep"), None, None),
            P(("shard", "rep"), None, None),
            P("shard", None),
            P("shard", None),
            P(None, "shard"),
            P("shard", None),
            P("shard", None),
            P(None, "shard"),
            P("shard", None),
            P("shard", None),
            P(None, "shard"),
            P("shard", None),
            P("shard", None),
            P(None, "shard"),
        ),
        check_vma=False,
    )
```

profile of v0, /device:TPU:0, one launch (start us, length us, event | category | flops | bytes accessed | tf_op | source)
XLA Modules:
  0.0 623.4 jit_solution(6696602671923517766)
XLA Ops:
  7.2 2.9 convert_element_type.95
  10.2 0.9 convert_element_type.105
  11.2 33.3 %all-gather = bf16[8,96,12]{1,2,0:T(8,128)(2,1)S(1)} all-gather(bf16[1,96,12]{1,2,0:T(8,128)(2,1)S(1)} %convert_bitcast_fusion.1), channel_id=1, replica_groups=mesh['shard'=8,'rep'=4] {'shard'}, dimensions={0}, use_global_device_ids=true | all-gather | bytes 20736 | tf_op jit(solution)/shard_map/all_gather | solution.py:223
  44.8 0.2 fusion.57
  45.1 105.8 %all-gather.4.cloned.1.call-done = bf16[768,6144]{1,0:T(8,128)(2,1)} async-done(((bf16[96,6144]{1,0:T(8,128)(2,1)}), bf16[768,6144]{1,0:T(8,128)(2,1)}) %all-gather.4.cloned.1.call-update) | async-done | bytes 9437200 | tf_op jit(solution)/shard_map/all_gather | solution.py:221
  150.9 3.0 fusion.10
  154.0 0.9 copy.63
  155.3 1.5 multiply_reduce_fusion.1
  156.9 0.5 exponential_reduce_fusion
  157.4 0.6 convolution_convert_fusion.4
  158.0 2.0 fusion.87
  160.3 5.4 multiply_convert_fusion.1
  165.7 1.0 copy-done.7
  166.7 3.7 convolution_convert_fusion
  170.7 60.5 %all-gather.6.cloned.1.call-done = bf16[3072,768]{1,0:T(8,128)(2,1)} async-done(((bf16[384,768]{1,0:T(8,128)(2,1)}), bf16[3072,768]{1,0:T(8,128)(2,1)}) %all-gather.6.cloned.1.call-update) | async-done | bytes 4718608 | tf_op jit(solution)/shard_map/all_gather | solution.py:222
  231.2 5.0 fusion.90
  236.2 4.7 multiply_reduce_fusion.2
  240.9 1.4 fusion.84
  242.3 2.5 convolution_convert_fusion.5
  244.8 1.9 copy.66
  246.7 2.5 convolution_convert_fusion.3
  249.2 2.4 copy.70
  251.6 3.0 fusion.91
  254.6 4.7 fusion.30
  259.3 4.9 fusion.86
  264.2 0.7 fusion.85
  264.9 0.7 copy-done.23
  265.6 1.3 convolution_convert_fusion.2
  267.1 1.6 convolution_convert_fusion.1
  268.7 4.2 pad_maximum_fusion
  272.9 0.3 reduce-scatter.10.cloned.1.call-start
  273.2 0.7 copy-done.15
  274.3 3.6 fusion.56
  278.0 0.8 copy.76
  278.9 50.0 %reduce-scatter.8.cloned.1.call-done = bf16[384,768]{1,0:T(8,128)(2,1)} async-done(((bf16[3072,768]{1,0:T(8,128)(2,1)}), bf16[384,768]{1,0:T(8,128)(2,1)}) %reduce-scatter.8.cloned.1.call-update) | async-done | bytes 589840 | tf_op jit(solution)/shard_map/reduce_scatter | solution.py:253
  328.9 165.2 %reduce-scatter.6.cloned.1.call-done = bf16[96,6144]{1,0:T(8,128)(2,1)} async-done(((bf16[768,6144]{1,0:T(8,128)(2,1)}), bf16[96,6144]{1,0:T(8,128)(2,1)}) %reduce-scatter.6.cloned.1.call-update) | async-done | bytes 1179664 | tf_op jit(solution)/shard_map/reduce_scatter | solution.py:239
  494.2 0.3 fusion.55
  494.4 1.4 copy.71
  495.9 4.3 fusion.37
  500.2 58.6 %reduce-scatter.10.cloned.1.call-done = bf16[96,12]{1,0:T(8,128)(2,1)} async-done(((bf16[768,12]{1,0:T(8,128)(2,1)}), bf16[96,12]{1,0:T(8,128)(2,1)}) %reduce-scatter.10.cloned.1.call-update) | async-done | bytes 2320
  558.8 0.8 copy.77
  559.6 5.7 psum.23
  565.3 0.6 multiply_subtract_fusion.2
  565.9 40.4 %all-reduce.3.cloned.1.call-done = (bf16[96,6144]{1,0:T(8,128)(2,1)}, bf16[384,768]{1,0:T(8,128)(2,1)}) async-done(((bf16[96,6144]{1,0:T(8,128)(2,1)}, bf16[384,768]{1,0:T(8,128)(2,1)}), (bf16[96,6144]{1,0:T(8,128)(2,1)}, bf16[384,768]{1,0:T(8,128)(2,1)})) %all-reduce.3.cloned.1.call-update) | async-done | bytes 1769488 | tf_op jit(solution)/shard_map/psum | solution.py:261
  606.3 4.6 multiply_subtract_fusion.1
  610.9 1.1 copy-done.17
  612.0 0.3 copy-done.22
  612.3 4.3 multiply_subtract_fusion
  (102 shorter events, 2.3 us)
Async XLA Ops:
  7.2 3.0 copy-start.3
  7.2 143.7 %all-gather.4.cloned.1.call-start = ((), (), s32[]{:S(2)}) async-start(), calls=%async_computation.3 | async-start | bytes 10616832 | tf_op jit(solution)/shard_map/all_gather | solution.py:221
  10.1 1.0 copy-start.25
  10.1 34.5 %copy-start.9 = (bf16[1,197,768]{2,1,0:T(8,128)(2,1)S(1)}, bf16[1,197,768]{2,1,0:T(8,128)(2,1)}, u32[]{:S(2)}) copy-start(bf16[1,197,768]{2,1,0:T(8,128)(2,1)} %param.11) | copy-start | bytes 907780
  10.2 221.0 %all-gather.6.cloned.1.call-start = ((), (), s32[]{:S(2)}) async-start(), calls=%async_computation.4 | async-start | bytes 5308416 | tf_op jit(solution)/shard_map/all_gather | solution.py:222
  11.1 317.8 %reduce-scatter.8.cloned.1.call-start = ((), (), s32[]{:S(2)}) async-start(), calls=%async_computation.6 | async-start | bytes 5308416 | tf_op jit(solution)/shard_map/reduce_scatter | solution.py:253
  155.1 2.2 copy-start.18
  156.8 1.1 copy-start.10
  158.0 2.3 copy-start.19
  160.0 76.2 %copy-start.1 = (f32[197,768]{1,0:T(8,128)}, f32[197,768]{1,0:T(8,128)S(1)}, u32[]{:S(2)}) copy-start(f32[197,768]{1,0:T(8,128)S(1)} %get-tuple-element.111) | copy-start | bytes 1815556
  160.3 6.4 %copy-start.13 = (bf16[1,197,768]{2,1,0:T(8,128)(2,1)S(1)}, bf16[1,197,768]{2,1,0:T(8,128)(2,1)}, u32[]{:S(2)}) copy-start(bf16[1,197,768]{2,1,0:T(8,128)(2,1)} %param.12) | copy-start | bytes 907780
  165.7 1.0 copy-start.7
  170.4 323.7 %reduce-scatter.6.cloned.1.call-start = ((), (), s32[]{:S(2)}) async-start(), calls=%async_computation.5 | async-start | bytes 10616832 | tf_op jit(solution)/shard_map/reduce_scatter | solution.py:239
  236.2 4.7 copy-start.20
  236.2 4.7 copy-start.14
  259.3 4.9 copy-start.6
  264.1 1.5 copy-start.11
  264.1 1.5 copy-start.28
  264.1 1.5 copy-start.30
  264.8 0.8 copy-start.23
  265.6 1.3 copy-start.2
  265.6 1.5 copy-start.21
  267.1 1.6 copy-start.5
  272.9 1.0 copy-start.15
  272.9 1.3 copy-start.12
  272.9 1.3 copy-start.24
  272.9 1.3 copy-start.29
  272.9 1.4 copy-start.31
  272.9 285.9 %reduce-scatter.10.cloned.1.call-start = ((), (), s32[]{:S(2)}) async-start(), calls=%async_computation.7 | async-start | bytes 221184
  278.9 327.5 %all-reduce.3.cloned.1.call-start = ((), (), s32[]{:S(2)}) async-start(), calls=%async_computation.8 | async-start | bytes 3538944 | tf_op jit(solution)/shard_map/psum | solution.py:261
  494.2 1.7 copy-start.8
  495.9 69.4 %copy-start.26 = (f32[12,96]{1,0:T(8,128)S(1)}, f32[12,96]{1,0:T(8,128)}, u32[]{:S(2)}) copy-start(f32[12,96]{1,0:T(8,128)} %param.18) | copy-start | bytes 13828
  495.9 69.4 %copy-start.27 = (f32[12,96]{1,0:T(8,128)S(1)}, f32[12,96]{1,0:T(8,128)}, u32[]{:S(2)}) copy-start(f32[12,96]{1,0:T(8,128)} %param.21) | copy-start | bytes 13828
  495.9 110.4 %copy-start.4 = (f32[384,768]{1,0:T(8,128)S(1)}, f32[384,768]{1,0:T(8,128)}, u32[]{:S(2)}) copy-start(f32[384,768]{1,0:T(8,128)} %param.14) | copy-start | bytes 3538948
  606.3 4.6 copy-start
  606.3 4.6 copy-start.16
  606.3 5.7 copy-start.17
  606.3 5.9 copy-start.22
Sparse Core Ops, SparseCore 0:
  10.8 140.0 all-gather.3
  153.6 77.5 all-gather.5
  234.9 94.0 reduce-scatter.7
  332.3 161.7 reduce-scatter.5
  497.8 60.9 reduce-scatter.9
  561.2 45.0 all-reduce.2
where the time goes:
time: 624 us; the launch traced here: 623 us
  waiting for transfers between devices  481 us (77%)
  matrix products  54.9 us (9%)
  blocking collectives  38.9 us (6%)
  other arithmetic  20.4 us (3%)
  between operations  14.6 us (2%)
  local copies, waits for them, and re-layouts  13.3 us (2%)
    reduce_scatter x1, waiting for transfers between devices, local(): lax.psum_scatter(jnp.concatenate([column_part(act_one, grad_proj), column...  165 us
    all_gather x1, waiting for transfers between devices, local(): lax.all_gather(halves[0], 'shard', axis=0, tiled=True)  106 us
    all_gather x1, waiting for transfers between devices, local(): lax.all_gather(halves[1], 'shard', axis=0, tiled=True)  60.5 us
    unnamed x7, waiting for transfers between devices  58.7 us
    reduce_scatter x1, waiting for transfers between devices, local(): lax.psum_scatter(grad_down_local.astype(jnp.bfloat16), 'shard', scatter_d...  50 us
    psum x1, waiting for transfers between devices, local(): lax.psum(owned_in, 'rep').astype(jnp.float32)  40.4 us
    all_gather x1, blocking collectives, local(): lax.all_gather(halves[2], 'shard', axis=1, tiled=True)  33.3 us
    dot_general x4, matrix products, times_transposed(): lax.dot_general(left, right, (((1,), (1,)), ((), ())), preferred_element_...  15.7 us
  transfers between devices with their start and end apart: 6, of which 6 were waited for; matrix products, arithmetic and copies ran while one was open for 12% of the time, Pallas kernels for 0%

commit v1 on v0

--- a/solution.py
+++ b/solution.py
@@ -13,6 +13,18 @@
 RATE_VECTOR = 0.15
 DECAY_MATRIX = 0.05
 STEP_COUNT = 2.0
+
+
+def collect(shard, axis, dim):
+    ways, here, hop = (lax.axis_size(axis), lax.axis_index(axis), shard.shape[dim])
+    dims = [n * ways if d == dim else n for d, n in enumerate(shard.shape)]
+    full = lax.dynamic_update_slice_in_dim(
+        jnp.zeros(dims, shard.dtype), shard, here * hop, axis=dim
+    )
+    for far in range(1, ways):
+        shard = lax.ppermute(shard, axis, [(d, (d + 1) % ways) for d in range(ways)])
+        full = lax.dynamic_update_slice_in_dim(full, shard, (here - far) % ways * hop, axis=dim)
+    return full
 
 
 def to_half(array_in):
@@ -219,7 +231,7 @@
     halves = (to_half(weights_in), to_half(weights_down), to_half(vectors))
     forward_set = (
         lax.all_gather(halves[0], "shard", axis=0, tiled=True),
-        lax.all_gather(halves[1], "shard", axis=0, tiled=True),
+        collect(halves[1], "shard", 0),
         lax.all_gather(halves[2], "shard", axis=1, tiled=True),
     )
     block_out, saved = forward_pass(images, forward_set[0], forward_set[1], forward_set[2])

time: 624 us -> 706 us (1.13)
  waiting for transfers between devices: 481 us -> 548 us
  local copies, waits for them, and re-layouts: 13.3 us -> 23.8 us
    ppermute x0 -> x7, waiting for transfers between devices: none -> 101 us  [collect(): lax.ppermute(shard, axis, [(d, (d + 1) % ways) for d in range(ways)])]
    reduce_scatter x1, waiting for transfers between devices: 50 us -> 19.6 us  [local(): lax.psum_scatter(grad_down_local.astype(jnp.bfloat16), 'shard', scatter_d...]
    dynamic_update_slice x0 -> x7, local copies, waits for them, and re-layouts: none -> 8.26 us  [collect(): lax.dynamic_update_slice_in_dim(full, shard, (here - far) % ways * hop, a...]
  transfers between devices with their start and end apart: 6 -> 13, of which waited for: 6 -> 13; matrix products, arithmetic and copies ran while one was open for 12% -> 12% of each run, Pallas kernels for 0% -> 0%
where the time goes in v1:
time: 706 us; the launch traced here: 705 us
  waiting for transfers between devices  548 us (78%)
  matrix products  55 us (8%)
  blocking collectives  39.1 us (6%)
  local copies, waits for them, and re-layouts  23.8 us (3%)
  other arithmetic  21 us (3%)
  between operations  14.6 us (2%)
    reduce_scatter x1, waiting for transfers between devices, local(): lax.psum_scatter(jnp.concatenate([column_part(act_one, grad_proj), column...  165 us
    all_gather x1, waiting for transfers between devices, local(): lax.all_gather(halves[0], 'shard', axis=0, tiled=True)  102 us
    ppermute x7, waiting for transfers between devices, collect(): lax.ppermute(shard, axis, [(d, (d + 1) % ways) for d in range(ways)])  101 us
    all_gather x1, waiting for transfers between devices, local(): lax.all_gather(halves[1], 'shard', axis=0, tiled=True)  60.5 us
    unnamed x7, waiting for transfers between devices  58.8 us
    psum x1, waiting for transfers between devices, local(): lax.psum(owned_in, 'rep').astype(jnp.float32)  40.4 us
    all_gather x1, blocking collectives, local(): lax.all_gather(halves[2], 'shard', axis=1, tiled=True)  33.5 us
    reduce_scatter x1, waiting for transfers between devices, local(): lax.psum_scatter(grad_down_local.astype(jnp.bfloat16), 'shard', scatter_d...  19.6 us
  transfers between devices with their start and end apart: 13, of which 13 were waited for; matrix products, arithmetic and copies ran while one was open for 12% of the time, Pallas kernels for 0%

profile of v1, /device:TPU:0, one launch (start us, length us, event | category | flops | bytes accessed | tf_op | source)
XLA Modules:
  0.0 705.2 jit_solution(8236575403257058351)
XLA Ops:
  7.2 2.8 convert_element_type.95
  10.4 0.9 copy-done.4
  11.3 0.9 constant_dynamic-update-slice_fusion.7
  12.2 2.2 copy-done.7
  14.6 33.5 %all-gather = bf16[8,96,12]{1,2,0:T(8,128)(2,1)S(1)} all-gather(bf16[1,96,12]{1,2,0:T(8,128)(2,1)S(1)} %convert_bitcast_fusion.1), channel_id=1, replica_groups=mesh['shard'=8,'rep'=4] {'shard'}, dimensions={0}, use_global_device_ids=true | all-gather | bytes 20736 | tf_op jit(solution)/shard_map/all_gather | solution.py:235
  48.6 102.4 %all-gather.4.cloned.1.call-done = bf16[768,6144]{1,0:T(8,128)(2,1)} async-done(((bf16[96,6144]{1,0:T(8,128)(2,1)}), bf16[768,6144]{1,0:T(8,128)(2,1)}) %all-gather.4.cloned.1.call-update) | async-done | bytes 9437200 | tf_op jit(solution)/shard_map/all_gather | solution.py:233
  151.0 3.0 fusion.10
  154.3 0.9 copy.63
  155.4 1.7 multiply_reduce_fusion.1
  158.2 2.0 fusion.87
  160.5 5.4 multiply_convert_fusion.1
  165.9 1.0 copy-done.9
  166.9 3.6 convolution_convert_fusion
  170.8 60.5 %all-gather.6.cloned.1.call-done = bf16[3072,768]{1,0:T(8,128)(2,1)} async-done(((bf16[384,768]{1,0:T(8,128)(2,1)}), bf16[3072,768]{1,0:T(8,128)(2,1)}) %all-gather.6.cloned.1.call-update) | async-done | bytes 4718608 | tf_op jit(solution)/shard_map/all_gather | solution.py:240
  231.3 5.0 fusion.90
  236.3 4.7 multiply_reduce_fusion.2
  241.0 1.4 fusion.84
  242.4 2.5 convolution_convert_fusion.5
  244.9 1.9 copy.66
  246.8 2.5 convolution_convert_fusion.3
  249.3 2.4 copy.70
  251.7 3.0 fusion.91
  254.7 4.7 fusion.30
  259.3 4.8 fusion.86
  265.7 1.3 convolution_convert_fusion.2
  267.2 1.6 convolution_convert_fusion.1
  268.8 4.2 pad_maximum_fusion
  273.0 1.0 copy-done.18
  274.8 21.0 %collective-permute-done = bf16[384,768]{1,0:T(8,128)(2,1)S(1)} collective-permute-done((bf16[384,768]{1,0:T(8,128)(2,1)S(1)}, bf16[384,768]{1,0:T(8,128)(2,1)S(1)}, u32[]{:S(2)}, u32[]{:S(2)}) %collective-permute-start) | collective-permute-done | bytes 589856 | tf_op jit(solution)/shard_map/ppermute | solution.py:25
  295.8 18.7 %collective-permute-done.1 = bf16[384,768]{1,0:T(8,128)(2,1)S(1)} collective-permute-done((bf16[384,768]{1,0:T(8,128)(2,1)S(1)}, bf16[384,768]{1,0:T(8,128)(2,1)S(1)}, u32[]{:S(2)}, u32[]{:S(2)}) %collective-permute-start.1) | collective-permute-done | bytes 589856 | tf_op jit(solution)/shard_map/ppermute | solution.py:25
  314.5 2.5 collective-permute-start.2
  316.9 13.4 %collective-permute-done.2 = bf16[384,768]{1,0:T(8,128)(2,1)S(1)} collective-permute-done((bf16[384,768]{1,0:T(8,128)(2,1)S(1)}, bf16[384,768]{1,0:T(8,128)(2,1)S(1)}, u32[]{:S(2)}, u32[]{:S(2)}) %collective-permute-start.2) | collective-permute-done | bytes 589856 | tf_op jit(solution)/shard_map/ppermute | solution.py:25
  330.3 15.0 %collective-permute-done.3 = bf16[384,768]{1,0:T(8,128)(2,1)S(1)} collective-permute-done((bf16[384,768]{1,0:T(8,128)(2,1)S(1)}, bf16[384,768]{1,0:T(8,128)(2,1)S(1)}, u32[]{:S(2)}, u32[]{:S(2)}) %collective-permute-start.3) | collective-permute-done | bytes 589856 | tf_op jit(solution)/shard_map/ppermute | solution.py:25
  345.3 14.2 %collective-permute-done.4 = bf16[384,768]{1,0:T(8,128)(2,1)} collective-permute-done((bf16[384,768]{1,0:T(8,128)(2,1)S(1)}, bf16[384,768]{1,0:T(8,128)(2,1)}, u32[]{:S(2)}, u32[]{:S(2)}) %collective-permute-start.4) | collective-permute-done | bytes 589856 | tf_op jit(solution)/shard_map/ppermute | solution.py:25
  360.5 12.6 %collective-permute-done.5 = bf16[384,768]{1,0:T(8,128)(2,1)} collective-permute-done((bf16[384,768]{1,0:T(8,128)(2,1)}, bf16[384,768]{1,0:T(8,128)(2,1)}, u32[]{:S(2)}, u32[]{:S(2)}) %collective-permute-start.5) | collective-permute-done | bytes 589856 | tf_op jit(solution)/shard_map/ppermute | solution.py:25
  375.7 2.0 constant_dynamic-update-slice_fusion.2
  377.7 2.0 constant_dynamic-update-slice_fusion.1
  379.7 6.2 collective-permute-done.6
  386.8 3.6 fusion.56
  391.6 19.6 %reduce-scatter.8.cloned.1.call-done = bf16[384,768]{1,0:T(8,128)(2,1)} async-done(((bf16[3072,768]{1,0:T(8,128)(2,1)}), bf16[384,768]{1,0:T(8,128)(2,1)}) %reduce-scatter.8.cloned.1.call-update) | async-done | bytes 589840 | tf_op jit(solution)/shard_map/reduce_scatter | solution.py:265
  411.1 165.2 %reduce-scatter.6.cloned.1.call-done = bf16[96,6144]{1,0:T(8,128)(2,1)} async-done(((bf16[768,6144]{1,0:T(8,128)(2,1)}), bf16[96,6144]{1,0:T(8,128)(2,1)}) %reduce-scatter.6.cloned.1.call-update) | async-done | bytes 1179664 | tf_op jit(solution)/shard_map/reduce_scatter | solution.py:251
  576.7 1.4 copy.71
  578.1 4.4 fusion.37
  582.5 58.7 %reduce-scatter.10.cloned.1.call-done = bf16[96,12]{1,0:T(8,128)(2,1)} async-done(((bf16[768,12]{1,0:T(8,128)(2,1)}), bf16[96,12]{1,0:T(8,128)(2,1)}) %reduce-scatter.10.cloned.1.call-update) | async-done | bytes 2320
  642.0 5.7 psum.23
  648.3 40.4 %all-reduce.3.cloned.1.call-done = (bf16[96,6144]{1,0:T(8,128)(2,1)}, bf16[384,768]{1,0:T(8,128)(2,1)}) async-done(((bf16[96,6144]{1,0:T(8,128)(2,1)}, bf16[384,768]{1,0:T(8,128)(2,1)}), (bf16[96,6144]{1,0:T(8,128)(2,1)}, bf16[384,768]{1,0:T(8,128)(2,1)})) %all-reduce.3.cloned.1.call-update) | async-done | bytes 1769488 | tf_op jit(solution)/shard_map/psum | solution.py:273
  688.7 7.2 %multiply_subtract_fusion = (f32[96,6144]{1,0:T(8,128)}, f32[96,6144]{1,0:T(8,128)}, f32[96,6144]{1,0:T(8,128)}, f32[96,6144]{1,0:T(8,128)}) fusion(f32[96,6144]{1,0:T(8,128)S(1)} %copy-done, f32[96,6144]{1,0:T(8,128)} %param.16, f32[96,6144]{1,0:T(8,128)} %param.19, bf16[96,6144]{1,0:T(8,128)(2,1)} %get-tuple-element.86), kind=kLoop, calls=%fused_computation.29 | loop fusion | flops 9437184 | bytes 17694720 | tf_op jit(solution)/shard_map/sub | solution.py:214
  695.9 2.4 multiply_subtract_fusion.1
  (130 shorter events, 12.9 us)
Async XLA Ops:
  7.2 143.8 %all-gather.4.cloned.1.call-start = ((), (), s32[]{:S(2)}) async-start(), calls=%async_computation.3 | async-start | bytes 10616832 | tf_op jit(solution)/shard_map/all_gather | solution.py:233
  10.1 1.3 copy-start.4
  10.1 221.2 %all-gather.6.cloned.1.call-start = ((), (), s32[]{:S(2)}) async-start(), calls=%async_computation.4 | async-start | bytes 5308416 | tf_op jit(solution)/shard_map/all_gather | solution.py:240
  11.3 3.2 copy-start.28
  11.3 36.9 %copy-start.11 = (bf16[1,197,768]{2,1,0:T(8,128)(2,1)S(1)}, bf16[1,197,768]{2,1,0:T(8,128)(2,1)}, u32[]{:S(2)}) copy-start(bf16[1,197,768]{2,1,0:T(8,128)(2,1)} %param.11) | copy-start | bytes 907780
  12.2 2.2 copy-start.7
  14.5 396.6 %reduce-scatter.8.cloned.1.call-start = ((), (), s32[]{:S(2)}) async-start(), calls=%async_computation.6 | async-start | bytes 5308416 | tf_op jit(solution)/shard_map/reduce_scatter | solution.py:265
  155.4 2.2 copy-start.19
  157.1 1.1 copy-start.12
  158.2 2.3 copy-start.20
  160.3 76.0 %copy-start.1 = (f32[197,768]{1,0:T(8,128)}, f32[197,768]{1,0:T(8,128)S(1)}, u32[]{:S(2)}) copy-start(f32[197,768]{1,0:T(8,128)S(1)} %get-tuple-element.113) | copy-start | bytes 1815556
  160.5 6.4 copy-start.15
  165.9 1.0 copy-start.9
  170.6 405.8 %reduce-scatter.6.cloned.1.call-start = ((), (), s32[]{:S(2)}) async-start(), calls=%async_computation.5 | async-start | bytes 10616832 | tf_op jit(solution)/shard_map/reduce_scatter | solution.py:251
  236.3 4.7 copy-start.21
  236.3 4.7 copy-start.16
  259.3 4.8 copy-start.8
  264.2 1.5 copy-start.13
  264.2 1.5 copy-start.31
  264.2 1.5 copy-start.33
  264.9 0.8 copy-start.26
  265.7 1.3 copy-start.2
  265.7 1.5 copy-start.22
  267.2 1.6 copy-start.6
  272.9 1.1 copy-start.18
  272.9 86.6 %copy-start.17 = (bf16[1,197,768]{2,1,0:T(8,128)(2,1)S(1)}, bf16[1,197,768]{2,1,0:T(8,128)(2,1)}, u32[]{:S(2)}) copy-start(bf16[1,197,768]{2,1,0:T(8,128)(2,1)} %param.12) | copy-start | bytes 907780
  273.0 368.2 %reduce-scatter.10.cloned.1.call-start = ((), (), s32[]{:S(2)}) async-start(), calls=%async_computation.7 | async-start | bytes 221184
  274.0 21.8 %collective-permute-start = (bf16[384,768]{1,0:T(8,128)(2,1)S(1)}, bf16[384,768]{1,0:T(8,128)(2,1)S(1)}, u32[]{:S(2)}, u32[]{:S(2)}) collective-permute-start(bf16[384,768]{1,0:T(8,128)(2,1)S(1)} %copy-done.18), channel_id=1, source_target_pairs={{0,4},{4,8},{8,12},{12,16},{16,20},{20,24},{24,28},{28,0},{1,5},{5... | collective-permute-start | bytes 1769480 | tf_op jit(solution)/shard_map/ppermute | solution.py:25
  295.8 18.7 %collective-permute-start.1 = (bf16[384,768]{1,0:T(8,128)(2,1)S(1)}, bf16[384,768]{1,0:T(8,128)(2,1)S(1)}, u32[]{:S(2)}, u32[]{:S(2)}) collective-permute-start(bf16[384,768]{1,0:T(8,128)(2,1)S(1)} %collective-permute-done), channel_id=1, source_target_pairs={{0,4},{4,8},{8,12},{12,16},{16,20},{20,24},{24,28},{28,0},{1,5},{5... | collective-permute-start | bytes 1769480 | tf_op jit(solution)/shard_map/ppermute | solution.py:25
  314.5 15.8 %collective-permute-start.2 = (bf16[384,768]{1,0:T(8,128)(2,1)S(1)}, bf16[384,768]{1,0:T(8,128)(2,1)S(1)}, u32[]{:S(2)}, u32[]{:S(2)}) collective-permute-start(bf16[384,768]{1,0:T(8,128)(2,1)S(1)} %collective-permute-done.1), channel_id=1, source_target_pairs={{0,4},{4,8},{8,12},{12,16},{16,20},{20,24},{24,28},{28,0},{1,5},{5... | collective-permute-start | bytes 1769480 | tf_op jit(solution)/shard_map/ppermute | solution.py:25
  330.3 15.0 %collective-permute-start.3 = (bf16[384,768]{1,0:T(8,128)(2,1)S(1)}, bf16[384,768]{1,0:T(8,128)(2,1)S(1)}, u32[]{:S(2)}, u32[]{:S(2)}) collective-permute-start(bf16[384,768]{1,0:T(8,128)(2,1)S(1)} %collective-permute-done.2), channel_id=1, source_target_pairs={{0,4},{4,8},{8,12},{12,16},{16,20},{20,24},{24,28},{28,0},{1,5},{5... | collective-permute-start | bytes 1769480 | tf_op jit(solution)/shard_map/ppermute | solution.py:25
  345.3 14.2 %collective-permute-start.4 = (bf16[384,768]{1,0:T(8,128)(2,1)S(1)}, bf16[384,768]{1,0:T(8,128)(2,1)}, u32[]{:S(2)}, u32[]{:S(2)}) collective-permute-start(bf16[384,768]{1,0:T(8,128)(2,1)S(1)} %collective-permute-done.3), channel_id=1, source_target_pairs={{0,4},{4,8},{8,12},{12,16},{16,20},{20,24},{24,28},{28,0},{1,5},{5... | collective-permute-start | bytes 1769480 | tf_op jit(solution)/shard_map/ppermute | solution.py:25
  359.5 13.6 %collective-permute-start.5 = (bf16[384,768]{1,0:T(8,128)(2,1)}, bf16[384,768]{1,0:T(8,128)(2,1)}, u32[]{:S(2)}, u32[]{:S(2)}) collective-permute-start(bf16[384,768]{1,0:T(8,128)(2,1)} %collective-permute-done.4), channel_id=1, source_target_pairs={{0,4},{4,8},{8,12},{12,16},{16,20},{20,24},{24,28},{28,0},{1,5},{5... | collective-permute-start | bytes 1769480 | tf_op jit(solution)/shard_map/ppermute | solution.py:25
  373.1 12.8 %collective-permute-start.6 = (bf16[384,768]{1,0:T(8,128)(2,1)}, bf16[384,768]{1,0:T(8,128)(2,1)S(1)}, u32[]{:S(2)}, u32[]{:S(2)}) collective-permute-start(bf16[384,768]{1,0:T(8,128)(2,1)} %collective-permute-done.5), channel_id=1, source_target_pairs={{0,4},{4,8},{8,12},{12,16},{16,20},{20,24},{24,28},{28,0},{1,5},{5... | collective-permute-start | bytes 1769480 | tf_op jit(solution)/shard_map/ppermute | solution.py:25
  374.9 11.9 %copy-start.14 = (bf16[1,197,768]{2,1,0:T(8,128)(2,1)S(1)}, bf16[1,197,768]{2,1,0:T(8,128)(2,1)}, u32[]{:S(2)}) copy-start(bf16[1,197,768]{2,1,0:T(8,128)(2,1)} %param.11) | copy-start | bytes 907780
  374.9 11.9 %copy-start.27 = (bf16[1,197,12,64]{1,3,2,0:T(8,128)(2,1)S(1)}, bf16[1,197,12,64]{1,3,2,0:T(8,128)(2,1)}, u32[]{:S(2)}) copy-start(bf16[1,197,12,64]{1,3,2,0:T(8,128)(2,1)} %copy-done.26) | copy-start | bytes 907780
  374.9 11.9 %copy-start.32 = (bf16[12,64,197]{2,1,0:T(8,128)(2,1)S(1)}, bf16[12,64,197]{2,1,0:T(8,128)(2,1)}, u32[]{:S(2)}) copy-start(bf16[12,64,197]{2,1,0:T(8,128)(2,1)} %fusion.30) | copy-start | bytes 907780
  374.9 11.9 %copy-start.34 = (bf16[1,197,12,64]{1,3,2,0:T(8,128)(2,1)S(1)}, bf16[1,197,12,64]{1,3,2,0:T(8,128)(2,1)}, u32[]{:S(2)}) copy-start(bf16[1,197,12,64]{1,3,2,0:T(8,128)(2,1)} %get-tuple-element.109) | copy-start | bytes 907780
  391.5 297.2 %all-reduce.3.cloned.1.call-start = ((), (), s32[]{:S(2)}) async-start(), calls=%async_computation.8 | async-start | bytes 3538944 | tf_op jit(solution)/shard_map/psum | solution.py:273
  576.4 1.7 copy-start.3
  576.4 1.7 copy-start.10
  578.1 69.5 %copy-start.29 = (f32[12,96]{1,0:T(8,128)S(1)}, f32[12,96]{1,0:T(8,128)}, u32[]{:S(2)}) copy-start(f32[12,96]{1,0:T(8,128)} %param.18) | copy-start | bytes 13828
  578.1 69.5 %copy-start.30 = (f32[12,96]{1,0:T(8,128)S(1)}, f32[12,96]{1,0:T(8,128)}, u32[]{:S(2)}) copy-start(f32[12,96]{1,0:T(8,128)} %param.21) | copy-start | bytes 13828
  578.1 110.5 %copy-start = (f32[96,6144]{1,0:T(8,128)S(1)}, f32[96,6144]{1,0:T(8,128)}, u32[]{:S(2)}) copy-start(f32[96,6144]{1,0:T(8,128)} %param.13) | copy-start | bytes 7077892
  688.7 7.2 %copy-start.5 = (f32[384,768]{1,0:T(8,128)S(1)}, f32[384,768]{1,0:T(8,128)}, u32[]{:S(2)}) copy-start(f32[384,768]{1,0:T(8,128)} %param.14) | copy-start | bytes 3538948
  688.7 7.2 %copy-start.23 = (f32[384,768]{1,0:T(8,128)S(1)}, f32[384,768]{1,0:T(8,128)}, u32[]{:S(2)}) copy-start(f32[384,768]{1,0:T(8,128)} %param.17) | copy-start | bytes 3538948
  688.7 7.2 %copy-start.24 = (f32[384,768]{1,0:T(8,128)S(1)}, f32[384,768]{1,0:T(8,128)}, u32[]{:S(2)}) copy-start(f32[384,768]{1,0:T(8,128)} %param.20) | copy-start | bytes 3538948
  688.7 7.2 %copy-start.25 = (bf16[384,768]{1,0:T(8,128)(2,1)S(1)}, bf16[384,768]{1,0:T(8,128)(2,1)}, u32[]{:S(2)}) copy-start(bf16[384,768]{1,0:T(8,128)(2,1)} %get-tuple-element.87) | copy-start | bytes 1769476
Sparse Core Ops, SparseCore 0:
  10.7 140.2 all-gather.3
  153.8 77.4 all-gather.5
  234.9 176.1 reduce-scatter.7
  414.6 161.7 reduce-scatter.5
  580.0 61.0 reduce-scatter.9
  643.6 45.0 all-reduce.2
